TPU v7x, 32 devices: a whole 2x2x4 slice. The times are simulated.
32 devices in a mesh: mom: 4 (over y, x), sec: 8 (over z, core).
Axes of the slice: x: 2, y: 2, z: 4, core: 2. Of those that a mesh axis runs over, the one named last changes fastest.
Arguments:
- left_env: bfloat16 [64, 64, 2816], P('sec', 'mom'), may hold values from -0.75 to 0.75
- right_env: bfloat16 [64, 64, 2816], P('sec', 'mom'), may hold values from -0.109375 to 0.109375
- left_mixed: bfloat16 [4, 64, 64, 2816], P('mom', 'sec'), may hold values from -0.75 to 0.75
- excitation: bfloat16 [4, 64, 64, 256], P('mom', 'sec'), may hold values from -6 to 6
- ground: bfloat16 [64, 64, 256], P('sec'), may hold values from -6 to 6
- mpo: bfloat16 [44, 4, 44, 4], replicated, may hold values from -0.4375 to 0.4375
- momentum: int32 [4], P('mom'), may hold values from 0 to 3, each once
- block_dims: int32 [64], P('sec'), may hold values from 16 to 64, as said below
Outputs:
- excited: bfloat16 [4, 2, 64, 64, 256], P('mom', None, 'sec')
Inputs may be any that keep to these rules, and one draw needn't show every extreme that they name: `block_dims`: every block has at least 16 used rows; some block uses all 64 and some exactly 16.
All inputs are finite; a program needn't handle non-finite values.
Results may differ from a plain program's by a relative error of at most 0.0058.
Values may be sent and summed in bfloat16 or wider, within the bound.
No kernel may reach another device: no remote copies, remote signals or barrier semaphores. Data moves between devices by JAX's collectives and lax.ppermute only.
A program may use at most 128 MiB of HBM per device.

v0:
```python
import math
import jax
import jax.numpy as jnp
from jax import lax
from jax.sharding import PartitionSpec as P


def with_halo(shard, sides, width):
    for axis, dim in sides:
        devices, length = (lax.axis_size(axis), shard.shape[dim])
        up = [(i, (i + 1) % devices) for i in range(devices - 1)]
        down = [(j, i) for i, j in up]
        last = lax.slice_in_dim(shard, length - width, length, axis=dim)
        initial = lax.slice_in_dim(shard, 0, width, axis=dim)
        before = lax.ppermute(last, axis, up)
        after = lax.ppermute(initial, axis, down)
        shard = jnp.concatenate([before, shard, after], axis=dim)
    return shard


def apply_term(left, source, right, mpo):
    width = left.shape[1]
    low = width // 3
    high = width - low
    bounds = [(0, low), (low, high), (high, width)]
    count = source.shape[0]
    rows = left.shape[0]
    block = right.shape[0]
    wide = source.shape[-1]
    phys = wide // block
    total = None
    for shift in range(3):
        start, stop = bounds[shift]
        temp = jnp.einsum(
            "iwa,nab->niwb",
            left[:, start:stop, :],
            source[:, shift],
            preferred_element_type=jnp.float32,
        ).astype(jnp.bfloat16)
        temp = temp.reshape(count, rows, stop - start, phys, block)
        part_sum = jnp.einsum(
            "niwpj,wpvq->nviqj", temp, mpo[start:stop], preferred_element_type=jnp.float32
        )
        total = part_sum if total is None else total + part_sum
    mixed = total.astype(jnp.bfloat16)
    result = jnp.einsum("nviqj,jvk->niqk", mixed, right, preferred_element_type=jnp.float32)
    return result.reshape(count, rows, wide)


def shards(left_env, right_env, left_mixed, excitation, ground, mpo, momentum, block_dims):
    sectors = excitation.shape[1]
    block = excitation.shape[2]
    wide = excitation.shape[3]
    width = left_env.shape[2] // block
    groups = lax.axis_size("mom")
    right_full = lax.all_gather(right_env, "mom", axis=1, tiled=True)
    stacked = jnp.stack([excitation[0], ground])
    padded = with_halo(stacked, (("sec", 1),), 1)
    sector_ids = jnp.arange(sectors, dtype=jnp.int32)

    def shifted_sector(sector):
        right = right_full[sector].reshape(block, width, block)
        mixl = left_mixed[0, sector].reshape(block, width, block)
        src = lax.dynamic_slice_in_dim(padded[1:2], sector, 3, 1)
        return apply_term(mixl, src, right, mpo)[0]

    shifted = lax.map(shifted_sector, sector_ids)
    left_full = lax.all_gather(left_env, "mom", axis=1, tiled=True)

    def direct_sector(sector):
        right = right_full[sector].reshape(block, width, block)
        left = left_full[sector].reshape(block, width, block)
        src = lax.dynamic_slice_in_dim(padded[0:1], sector, 3, 1)
        return apply_term(left, src, right, mpo)[0]

    direct = lax.map(direct_sector, sector_ids)
    phase = 2.0 * math.pi * momentum[0].astype(jnp.float32) / groups
    rows_idx = jnp.arange(block, dtype=jnp.int32)
    cols_idx = jnp.arange(wide, dtype=jnp.int32) % block
    used = block_dims[:, None, None]
    mask = ((rows_idx[None, :, None] < used) & (cols_idx[None, None, :] < used)).astype(jnp.float32)
    real_part = mask * (direct + jnp.cos(phase) * shifted)
    imag_part = -mask * jnp.sin(phase) * shifted
    return jnp.stack([real_part, imag_part])[None].astype(jnp.bfloat16)


def solution(mesh):
    return jax.shard_map(
        shards,
        mesh=mesh,
        in_specs=(
            P("sec", "mom", None),
            P("sec", "mom", None),
            P("mom", "sec", None, None),
            P("mom", "sec", None, None),
            P("sec", None, None),
            P(),
            P("mom"),
            P("sec"),
        ),
        out_specs=P("mom", None, "sec", None, None),
        check_vma=False,
    )
```

profile of v0, /device:TPU:0, one launch (start us, length us, event | category | flops | bytes accessed | tf_op | source)
XLA Modules:
  0.0 640.0 jit_solution(17581412542030367887)
XLA Ops:
  18.7 35.0 %all-gather.3.cloned.1.call-done = bf16[8,64,2816]{2,1,0:T(8,128)(2,1)} async-done(((bf16[8,16,2816]{2,1,0:T(8,128)(2,1)}), bf16[8,64,2816]{2,1,0:T(8,128)(2,1)}) %all-gather.3.cloned.1.call-update) | async-done | bytes 2883600 | tf_op jit(solution)/shard_map/all_gather | solution.py:68
  53.7 43.7 %all-gather.5.cloned.1.call-done = bf16[8,64,2816]{2,1,0:T(8,128)(2,1)} async-done(((bf16[8,16,2816]{2,1,0:T(8,128)(2,1)}), bf16[8,64,2816]{2,1,0:T(8,128)(2,1)}) %all-gather.5.cloned.1.call-update) | async-done | bytes 2883600 | tf_op jit(solution)/shard_map/all_gather | solution.py:56
  98.3 268.4 %while.20 = (s32[]{:T(128)}, f32[8,64,256]{2,1,0:T(8,128)}, bf16[2,10,64,256]{3,2,1,0:T(8,128)(2,1)S(1)}, s32[8]{0:T(128)S(1)}, bf16[8,64,2816]{2,1,0:T(8,128)(2...) while((s32[]{:T(128)}, f32[8,64,256]{2,1,0:T(8,128)}, ...), condition=%wide.region_1.2_spmd, body=%wide.region_0.1_spmd.sunk | while | flops 441188352 | bytes 44241284 | solution.py:76
  115.9 6.3 fusion.110
  122.3 5.2 copy.125
  149.5 6.3 fusion.110
  155.8 5.2 copy.125
  183.0 6.3 fusion.110
  216.6 6.3 fusion.110
  222.9 5.2 copy.125
  250.1 6.3 fusion.110
  256.5 5.2 copy.125
  283.7 6.3 fusion.110
  317.3 6.3 fusion.110
  350.8 6.3 fusion.110
  367.5 263.4 %while.21 = (s32[]{:T(128)}, f32[8,64,256]{2,1,0:T(8,128)}, bf16[2,10,64,256]{3,2,1,0:T(8,128)(2,1)S(1)}, s32[8]{0:T(128)S(1)}, bf16[1,8,64,2816]{3,2,1,0:T(8,12...) while((s32[]{:T(128)}, f32[8,64,256]{2,1,0:T(8,128)}, ...), condition=%wide.region_3.4_spmd, body=%wide.region_2.3_spmd.sunk | while | flops 441188352 | bytes 43225452 | solution.py:67
  383.5 6.3 fusion.128
  416.4 6.3 fusion.128
  449.3 6.3 fusion.128
  482.3 6.3 fusion.128
  515.2 6.3 fusion.128
  548.1 6.3 fusion.128
  581.1 6.3 fusion.128
  614.0 6.3 fusion.128
  (492 shorter events, 372.1 us)
Async XLA Ops:
  6.5 47.2 %all-gather.3.cloned.1.call-start = ((), (), s32[]{:S(2)}) async-start(), calls=%async_computation | async-start | bytes 3604480 | tf_op jit(solution)/shard_map/all_gather | solution.py:68
  7.3 90.2 %all-gather.5.cloned.1.call-start = ((), (), s32[]{:S(2)}) async-start(), calls=%async_computation.1 | async-start | bytes 3604480 | tf_op jit(solution)/shard_map/all_gather | solution.py:56
  8.8 8.7 %collective-permute-start.1 = (bf16[2,1,64,256]{3,2,1,0:T(8,128)(2,1)S(1)}, bf16[2,1,64,256]{3,2,1,0:T(8,128)(2,1)S(1)}, u32[]{:S(2)}, u32[]{:S(2)}) collective-permute-start(bf16[2,1,64,256]{3,2,1,0:T(8,128)(2,1)S(1)} %get-tuple-element.146), channel_id=1, source_target_pairs={{1,0},{2,1},{3,2},{4,3},{5,4},{6,5},{7,6},{9,8},{10,9},{11,10},{12... | collective-permute-start | bytes 196616 | tf_op jit(solution)/shard_map/ppermute | solution.py:16
  10.1 7.4 %collective-permute-start = (bf16[2,1,64,256]{3,2,1,0:T(8,128)(2,1)S(1)}, bf16[2,1,64,256]{3,2,1,0:T(8,128)(2,1)S(1)}, u32[]{:S(2)}, u32[]{:S(2)}) collective-permute-start(bf16[2,1,64,256]{3,2,1,0:T(8,128)(2,1)S(1)} %get-tuple-element.145), channel_id=1, source_target_pairs={{0,1},{1,2},{2,3},{3,4},{4,5},{5,6},{6,7},{8,9},{9,10},{10,11},{11... | collective-permute-start | bytes 196616 | tf_op jit(solution)/shard_map/ppermute | solution.py:15
  98.3 11.6 %copy-start = (bf16[44,4,44,4]{2,0,1,3:T(8,128)(2,1)}, bf16[44,4,44,4]{2,0,1,3:T(8,128)(2,1)S(1)}, u32[]{:S(2)}) copy-start(bf16[44,4,44,4]{2,0,1,3:T(8,128)(2,1)S(1)} %get-tuple-element.276) | copy-start | bytes 185860 | tf_op jit(solution)/shard_map/while
  131.8 5.7 copy-start.4
  131.8 11.6 %copy-start = (bf16[44,4,44,4]{2,0,1,3:T(8,128)(2,1)}, bf16[44,4,44,4]{2,0,1,3:T(8,128)(2,1)S(1)}, u32[]{:S(2)}) copy-start(bf16[44,4,44,4]{2,0,1,3:T(8,128)(2,1)S(1)} %get-tuple-element.276) | copy-start | bytes 185860 | tf_op jit(solution)/shard_map/while
  165.4 5.7 copy-start.4
  165.4 11.6 %copy-start = (bf16[44,4,44,4]{2,0,1,3:T(8,128)(2,1)}, bf16[44,4,44,4]{2,0,1,3:T(8,128)(2,1)S(1)}, u32[]{:S(2)}) copy-start(bf16[44,4,44,4]{2,0,1,3:T(8,128)(2,1)S(1)} %get-tuple-element.276) | copy-start | bytes 185860 | tf_op jit(solution)/shard_map/while
  198.9 11.6 %copy-start = (bf16[44,4,44,4]{2,0,1,3:T(8,128)(2,1)}, bf16[44,4,44,4]{2,0,1,3:T(8,128)(2,1)S(1)}, u32[]{:S(2)}) copy-start(bf16[44,4,44,4]{2,0,1,3:T(8,128)(2,1)S(1)} %get-tuple-element.276) | copy-start | bytes 185860 | tf_op jit(solution)/shard_map/while
  232.5 11.6 %copy-start = (bf16[44,4,44,4]{2,0,1,3:T(8,128)(2,1)}, bf16[44,4,44,4]{2,0,1,3:T(8,128)(2,1)S(1)}, u32[]{:S(2)}) copy-start(bf16[44,4,44,4]{2,0,1,3:T(8,128)(2,1)S(1)} %get-tuple-element.276) | copy-start | bytes 185860 | tf_op jit(solution)/shard_map/while
  266.0 11.6 %copy-start = (bf16[44,4,44,4]{2,0,1,3:T(8,128)(2,1)}, bf16[44,4,44,4]{2,0,1,3:T(8,128)(2,1)S(1)}, u32[]{:S(2)}) copy-start(bf16[44,4,44,4]{2,0,1,3:T(8,128)(2,1)S(1)} %get-tuple-element.276) | copy-start | bytes 185860 | tf_op jit(solution)/shard_map/while
  299.6 11.6 %copy-start = (bf16[44,4,44,4]{2,0,1,3:T(8,128)(2,1)}, bf16[44,4,44,4]{2,0,1,3:T(8,128)(2,1)S(1)}, u32[]{:S(2)}) copy-start(bf16[44,4,44,4]{2,0,1,3:T(8,128)(2,1)S(1)} %get-tuple-element.276) | copy-start | bytes 185860 | tf_op jit(solution)/shard_map/while
  333.2 11.6 %copy-start = (bf16[44,4,44,4]{2,0,1,3:T(8,128)(2,1)}, bf16[44,4,44,4]{2,0,1,3:T(8,128)(2,1)S(1)}, u32[]{:S(2)}) copy-start(bf16[44,4,44,4]{2,0,1,3:T(8,128)(2,1)S(1)} %get-tuple-element.276) | copy-start | bytes 185860 | tf_op jit(solution)/shard_map/while
  367.5 263.4 %copy-start.9 = (pred[8,256]{1,0:T(8,128)(4,1)S(1)}, pred[8,256]{1,0:T(8,128)(4,1)}, u32[]{:S(2)}) copy-start(pred[8,256]{1,0:T(8,128)(4,1)} %broadcast_compare_fusion) | copy-start | bytes 6148
  367.5 263.4 %copy-start.10 = (pred[8,64]{1,0:T(8,128)(4,1)S(1)}, pred[8,64]{1,0:T(8,128)(4,1)}, u32[]{:S(2)}) copy-start(pred[8,64]{1,0:T(8,128)(4,1)} %iota_compare_fusion) | copy-start | bytes 1540
  367.5 10.7 %copy-start.2 = (bf16[44,4,44,4]{2,0,1,3:T(8,128)(2,1)}, bf16[44,4,44,4]{2,0,1,3:T(8,128)(2,1)S(1)}, u32[]{:S(2)}) copy-start(bf16[44,4,44,4]{2,0,1,3:T(8,128)(2,1)S(1)} %get-tuple-element.315) | copy-start | bytes 185860 | tf_op jit(solution)/shard_map/while
  400.4 10.8 %copy-start.2 = (bf16[44,4,44,4]{2,0,1,3:T(8,128)(2,1)}, bf16[44,4,44,4]{2,0,1,3:T(8,128)(2,1)S(1)}, u32[]{:S(2)}) copy-start(bf16[44,4,44,4]{2,0,1,3:T(8,128)(2,1)S(1)} %get-tuple-element.315) | copy-start | bytes 185860 | tf_op jit(solution)/shard_map/while
  433.3 10.8 %copy-start.2 = (bf16[44,4,44,4]{2,0,1,3:T(8,128)(2,1)}, bf16[44,4,44,4]{2,0,1,3:T(8,128)(2,1)S(1)}, u32[]{:S(2)}) copy-start(bf16[44,4,44,4]{2,0,1,3:T(8,128)(2,1)S(1)} %get-tuple-element.315) | copy-start | bytes 185860 | tf_op jit(solution)/shard_map/while
  466.2 10.8 %copy-start.2 = (bf16[44,4,44,4]{2,0,1,3:T(8,128)(2,1)}, bf16[44,4,44,4]{2,0,1,3:T(8,128)(2,1)S(1)}, u32[]{:S(2)}) copy-start(bf16[44,4,44,4]{2,0,1,3:T(8,128)(2,1)S(1)} %get-tuple-element.315) | copy-start | bytes 185860 | tf_op jit(solution)/shard_map/while
  499.2 10.8 %copy-start.2 = (bf16[44,4,44,4]{2,0,1,3:T(8,128)(2,1)}, bf16[44,4,44,4]{2,0,1,3:T(8,128)(2,1)S(1)}, u32[]{:S(2)}) copy-start(bf16[44,4,44,4]{2,0,1,3:T(8,128)(2,1)S(1)} %get-tuple-element.315) | copy-start | bytes 185860 | tf_op jit(solution)/shard_map/while
  532.1 10.8 %copy-start.2 = (bf16[44,4,44,4]{2,0,1,3:T(8,128)(2,1)}, bf16[44,4,44,4]{2,0,1,3:T(8,128)(2,1)S(1)}, u32[]{:S(2)}) copy-start(bf16[44,4,44,4]{2,0,1,3:T(8,128)(2,1)S(1)} %get-tuple-element.315) | copy-start | bytes 185860 | tf_op jit(solution)/shard_map/while
  565.0 10.8 %copy-start.2 = (bf16[44,4,44,4]{2,0,1,3:T(8,128)(2,1)}, bf16[44,4,44,4]{2,0,1,3:T(8,128)(2,1)S(1)}, u32[]{:S(2)}) copy-start(bf16[44,4,44,4]{2,0,1,3:T(8,128)(2,1)S(1)} %get-tuple-element.315) | copy-start | bytes 185860 | tf_op jit(solution)/shard_map/while
  598.0 10.8 %copy-start.2 = (bf16[44,4,44,4]{2,0,1,3:T(8,128)(2,1)}, bf16[44,4,44,4]{2,0,1,3:T(8,128)(2,1)S(1)}, u32[]{:S(2)}) copy-start(bf16[44,4,44,4]{2,0,1,3:T(8,128)(2,1)S(1)} %get-tuple-element.315) | copy-start | bytes 185860 | tf_op jit(solution)/shard_map/while
  (54 other events, 232.5 us)
Sparse Core Ops, SparseCore 0:
  9.2 44.4 all-gather.2
  55.6 41.7 all-gather.4
where the time goes:
time: 643 us; the launch traced here: 640 us
  matrix products  291 us (45%)
  local copies, waits for them, and re-layouts  191 us (30%)
  waiting for transfers between devices  80.1 us (12%)
  loops' own time  52.6 us (8%)
  between operations  14.3 us (2%)
  other arithmetic  6.82 us (1%)
    dot_general x48, matrix products, apply_term(): jnp.einsum('niwpj,wpvq->nviqj', temp, mpo[start:stop], preferred_element_...  220 us
    another operation x66, local copies, waits for them, and re-layouts  119 us
    dot_general x16, matrix products, apply_term(): jnp.einsum('nviqj,jvk->niqk', mixed, right, preferred_element_type=jnp.fl...  46.1 us
    all_gather x1, waiting for transfers between devices, shards(): right_full = lax.all_gather(right_env, 'mom', axis=1, tiled=True)  43.7 us
    all_gather x1, waiting for transfers between devices, shards(): left_full = lax.all_gather(left_env, 'mom', axis=1, tiled=True)  35 us
    another operation x1, loops' own time, shards(): shifted = lax.map(shifted_sector, sector_ids)  26.6 us
    another operation x1, loops' own time, shards(): direct = lax.map(direct_sector, sector_ids)  26 us
    dot_general x48, matrix products, apply_term(): jnp.einsum('iwa,nab->niwb', left[:, start:stop, :], source[:, shift], pre...  25 us
  transfers between devices with their start and end apart: 4, of which 2 were waited for; matrix products, arithmetic and copies ran while one was open for 1% of the time, Pallas kernels for 0%

commit v1 on v0

--- a/solution.py
+++ b/solution.py
@@ -3,6 +3,16 @@
 import jax.numpy as jnp
 from jax import lax
 from jax.sharding import PartitionSpec as P
+
+
+def turned_line(block, axis, d):
+    size = lax.axis_size(axis)
+    held, shards = (block, [block])
+    for _ in range(size - 1):
+        held = lax.ppermute(held, axis, [(i, (i + 1) % size) for i in range(size)])
+        shards.insert(0, held)
+    flat = jnp.concatenate(shards, axis=d)
+    return jnp.roll(flat, (lax.axis_index(axis) + 1) * block.shape[d], axis=d)
 
 
 def with_halo(shard, sides, width):
@@ -53,7 +63,7 @@
     wide = excitation.shape[3]
     width = left_env.shape[2] // block
     groups = lax.axis_size("mom")
-    right_full = lax.all_gather(right_env, "mom", axis=1, tiled=True)
+    right_full = turned_line(right_env, "mom", 1)
     stacked = jnp.stack([excitation[0], ground])
     padded = with_halo(stacked, (("sec", 1),), 1)
     sector_ids = jnp.arange(sectors, dtype=jnp.int32)

time: 643 us -> 630 us (0.980)
  waiting for transfers between devices: 80.1 us -> 40.9 us
  matrix products: 291 us -> 306 us
    all_gather x1 -> x0, waiting for transfers between devices: 43.7 us -> none  [shards(): right_full = lax.all_gather(right_env, 'mom', axis=1, tiled=True)]
    ppermute x0 -> x3, waiting for transfers between devices: none -> 40.9 us  [turned_line(): held = lax.ppermute(held, axis, [(i, (i + 1) % size) for i in range(size)])]
    all_gather x1, waiting for transfers between devices: 35 us -> 0.01 us  [shards(): left_full = lax.all_gather(left_env, 'mom', axis=1, tiled=True)]
    dot_general x48, matrix products: 220 us -> 247 us  [apply_term(): jnp.einsum('niwpj,wpvq->nviqj', temp, mpo[start:stop], preferred_element_...]
    dot_general x48, matrix products: 25 us -> 12.9 us  [apply_term(): jnp.einsum('iwa,nab->niwb', left[:, start:stop, :], source[:, shift], pre...]
  transfers between devices with their start and end apart: 4 -> 6, of which waited for: 2 -> 3; matrix products, arithmetic and copies ran while one was open for 1% -> 42% of each run, Pallas kernels for 0% -> 0%
where the time goes in v1:
time: 630 us; the launch traced here: 626 us
  matrix products  306 us (49%)
  local copies, waits for them, and re-layouts  197 us (31%)
  loops' own time  52.6 us (8%)
  waiting for transfers between devices  40.9 us (6%)
  between operations  14.3 us (2%)
  starting transfers between devices  7.99 us (1%)
  other arithmetic  6.86 us (1%)
    dot_general x48, matrix products, apply_term(): jnp.einsum('niwpj,wpvq->nviqj', temp, mpo[start:stop], preferred_element_...  247 us
    another operation x66, local copies, waits for them, and re-layouts  118 us
    dot_general x16, matrix products, apply_term(): jnp.einsum('nviqj,jvk->niqk', mixed, right, preferred_element_type=jnp.fl...  46.1 us
    ppermute x3, waiting for transfers between devices, turned_line(): held = lax.ppermute(held, axis, [(i, (i + 1) % size) for i in range(size)])  40.9 us
    another operation x1, loops' own time, shards(): shifted = lax.map(shifted_sector, sector_ids)  26.3 us
    another operation x1, loops' own time, shards(): direct = lax.map(direct_sector, sector_ids)  26.3 us
    dot_general x48, matrix products, apply_term(): jnp.einsum('iwa,nab->niwb', left[:, start:stop, :], source[:, shift], pre...  12.9 us
  transfers between devices with their start and end apart: 6, of which 3 were waited for; matrix products, arithmetic and copies ran while one was open for 42% of the time, Pallas kernels for 0%

profile of v1, /device:TPU:0, one launch (start us, length us, event | category | flops | bytes accessed | tf_op | source)
XLA Modules:
  0.0 626.0 jit_solution(1470597375782306989)
XLA Ops:
  9.5 17.4 %collective-permute-done.2 = bf16[8,16,2816]{2,1,0:T(8,128)(2,1)S(1)} collective-permute-done((bf16[8,16,2816]{2,1,0:T(8,128)(2,1)}, bf16[8,16,2816]{2,1,0:T(8,128)(2,1)S(1)}, u32[]{:S(2)}, u32[]{:S(2)}) %collective-permute-start.2) | collective-permute-done | bytes 720928 | tf_op jit(solution)/shard_map/ppermute | solution.py:12
  27.6 17.5 %collective-permute-done.3 = bf16[8,16,2816]{2,1,0:T(8,128)(2,1)S(1)} collective-permute-done((bf16[8,16,2816]{2,1,0:T(8,128)(2,1)S(1)}, bf16[8,16,2816]{2,1,0:T(8,128)(2,1)S(1)}, u32[]{:S(2)}, u32[]{:S(2)}) %collective-permute-start.3) | collective-permute-done | bytes 720928 | tf_op jit(solution)/shard_map/ppermute | solution.py:12
  56.5 6.0 collective-permute-done.4
  67.8 277.9 %while.21 = (s32[]{:T(128)}, f32[8,64,256]{2,1,0:T(8,128)}, bf16[2,10,64,256]{3,2,1,0:T(8,128)(2,1)S(1)}, s32[8]{0:T(128)S(1)}, bf16[1,8,64,2816]{3,2,1,0:T(8,12...) while((s32[]{:T(128)}, f32[8,64,256]{2,1,0:T(8,128)}, ...), condition=%wide.region_3.4_spmd, body=%wide.region_2.3_spmd.sunk | while | flops 441188352 | bytes 41746740 | solution.py:77
  85.6 6.3 %fusion.128 = bf16[44,64,4,64]{3,0,2,1:T(8,128)(2,1)S(1)} fusion(f32[64,64,44,4,1]{1,2,4,3,0:T(8,128)} %fusion.123, f32[64,64,44,4,1]{1,2,4,3,0:T(8,128)} %fusion.126, bf16[64,14,4,64,1]{3,2,0,1,4:T(4,128)(2,1)} %bitcast.261, bf16[44,4,44,4]{2,0,1,3:T(8,128)(2,1)} %get-tuple-element.315), kind=kOutput, calls=%fused_computation.38.clone.1 | convolution fusion | flops 82903040 | bytes 15007744 | tf_op jit(solution)/shard_map/while/body/eval_jaxpr/niwpj,wpvq->nviqj/dot_general | solution.py:51
  91.9 5.2 copy.133
  120.3 6.3 %fusion.128 = bf16[44,64,4,64]{3,0,2,1:T(8,128)(2,1)S(1)} fusion(f32[64,64,44,4,1]{1,2,4,3,0:T(8,128)} %fusion.123, f32[64,64,44,4,1]{1,2,4,3,0:T(8,128)} %fusion.126, bf16[64,14,4,64,1]{3,2,0,1,4:T(4,128)(2,1)} %bitcast.261, bf16[44,4,44,4]{2,0,1,3:T(8,128)(2,1)} %get-tuple-element.315), kind=kOutput, calls=%fused_computation.38.clone.1 | convolution fusion | flops 82903040 | bytes 15007744 | tf_op jit(solution)/shard_map/while/body/eval_jaxpr/niwpj,wpvq->nviqj/dot_general | solution.py:51
  126.7 5.2 copy.133
  155.0 6.3 %fusion.128 = bf16[44,64,4,64]{3,0,2,1:T(8,128)(2,1)S(1)} fusion(f32[64,64,44,4,1]{1,2,4,3,0:T(8,128)} %fusion.123, f32[64,64,44,4,1]{1,2,4,3,0:T(8,128)} %fusion.126, bf16[64,14,4,64,1]{3,2,0,1,4:T(4,128)(2,1)} %bitcast.261, bf16[44,4,44,4]{2,0,1,3:T(8,128)(2,1)} %get-tuple-element.315), kind=kOutput, calls=%fused_computation.38.clone.1 | convolution fusion | flops 82903040 | bytes 15007744 | tf_op jit(solution)/shard_map/while/body/eval_jaxpr/niwpj,wpvq->nviqj/dot_general | solution.py:51
  161.4 5.2 copy.133
  189.8 6.3 %fusion.128 = bf16[44,64,4,64]{3,0,2,1:T(8,128)(2,1)S(1)} fusion(f32[64,64,44,4,1]{1,2,4,3,0:T(8,128)} %fusion.123, f32[64,64,44,4,1]{1,2,4,3,0:T(8,128)} %fusion.126, bf16[64,14,4,64,1]{3,2,0,1,4:T(4,128)(2,1)} %bitcast.261, bf16[44,4,44,4]{2,0,1,3:T(8,128)(2,1)} %get-tuple-element.315), kind=kOutput, calls=%fused_computation.38.clone.1 | convolution fusion | flops 82903040 | bytes 15007744 | tf_op jit(solution)/shard_map/while/body/eval_jaxpr/niwpj,wpvq->nviqj/dot_general | solution.py:51
  224.5 6.3 %fusion.128 = bf16[44,64,4,64]{3,0,2,1:T(8,128)(2,1)S(1)} fusion(f32[64,64,44,4,1]{1,2,4,3,0:T(8,128)} %fusion.123, f32[64,64,44,4,1]{1,2,4,3,0:T(8,128)} %fusion.126, bf16[64,14,4,64,1]{3,2,0,1,4:T(4,128)(2,1)} %bitcast.261, bf16[44,4,44,4]{2,0,1,3:T(8,128)(2,1)} %get-tuple-element.315), kind=kOutput, calls=%fused_computation.38.clone.1 | convolution fusion | flops 82903040 | bytes 15007744 | tf_op jit(solution)/shard_map/while/body/eval_jaxpr/niwpj,wpvq->nviqj/dot_general | solution.py:51
  259.3 6.3 %fusion.128 = bf16[44,64,4,64]{3,0,2,1:T(8,128)(2,1)S(1)} fusion(f32[64,64,44,4,1]{1,2,4,3,0:T(8,128)} %fusion.123, f32[64,64,44,4,1]{1,2,4,3,0:T(8,128)} %fusion.126, bf16[64,14,4,64,1]{3,2,0,1,4:T(4,128)(2,1)} %bitcast.261, bf16[44,4,44,4]{2,0,1,3:T(8,128)(2,1)} %get-tuple-element.315), kind=kOutput, calls=%fused_computation.38.clone.1 | convolution fusion | flops 82903040 | bytes 15007744 | tf_op jit(solution)/shard_map/while/body/eval_jaxpr/niwpj,wpvq->nviqj/dot_general | solution.py:51
  294.0 6.3 %fusion.128 = bf16[44,64,4,64]{3,0,2,1:T(8,128)(2,1)S(1)} fusion(f32[64,64,44,4,1]{1,2,4,3,0:T(8,128)} %fusion.123, f32[64,64,44,4,1]{1,2,4,3,0:T(8,128)} %fusion.126, bf16[64,14,4,64,1]{3,2,0,1,4:T(4,128)(2,1)} %bitcast.261, bf16[44,4,44,4]{2,0,1,3:T(8,128)(2,1)} %get-tuple-element.315), kind=kOutput, calls=%fused_computation.38.clone.1 | convolution fusion | flops 82903040 | bytes 15007744 | tf_op jit(solution)/shard_map/while/body/eval_jaxpr/niwpj,wpvq->nviqj/dot_general | solution.py:51
  328.7 6.3 %fusion.128 = bf16[44,64,4,64]{3,0,2,1:T(8,128)(2,1)S(1)} fusion(f32[64,64,44,4,1]{1,2,4,3,0:T(8,128)} %fusion.123, f32[64,64,44,4,1]{1,2,4,3,0:T(8,128)} %fusion.126, bf16[64,14,4,64,1]{3,2,0,1,4:T(4,128)(2,1)} %bitcast.261, bf16[44,4,44,4]{2,0,1,3:T(8,128)(2,1)} %get-tuple-element.315), kind=kOutput, calls=%fused_computation.38.clone.1 | convolution fusion | flops 82903040 | bytes 15007744 | tf_op jit(solution)/shard_map/while/body/eval_jaxpr/niwpj,wpvq->nviqj/dot_general | solution.py:51
  346.5 270.3 %while.20 = (s32[]{:T(128)}, f32[8,64,256]{2,1,0:T(8,128)}, bf16[2,10,64,256]{3,2,1,0:T(8,128)(2,1)S(1)}, s32[8]{0:T(128)S(1)}, bf16[8,64,2816]{2,1,0:T(8,128)(2...) while((s32[]{:T(128)}, f32[8,64,256]{2,1,0:T(8,128)}, ...), condition=%wide.region_1.2_spmd, body=%wide.region_0.1_spmd.sunk | while | flops 441188352 | bytes 41746736 | solution.py:86
  364.3 6.3 %fusion.110 = bf16[44,64,4,64]{3,0,2,1:T(8,128)(2,1)S(1)} fusion(f32[64,64,44,4,1]{1,2,4,3,0:T(8,128)} %fusion.105, f32[64,64,44,4,1]{1,2,4,3,0:T(8,128)} %fusion.108, bf16[64,14,4,64,1]{3,2,0,1,4:T(4,128)(2,1)} %bitcast.262, bf16[44,4,44,4]{2,0,1,3:T(8,128)(2,1)} %get-tuple-element.276), kind=kOutput, calls=%fused_computation.3.clone.1 | convolution fusion | flops 82903040 | bytes 15007744 | tf_op jit(solution)/shard_map/while/body/eval_jaxpr/niwpj,wpvq->nviqj/dot_general | solution.py:51
  398.1 6.3 %fusion.110 = bf16[44,64,4,64]{3,0,2,1:T(8,128)(2,1)S(1)} fusion(f32[64,64,44,4,1]{1,2,4,3,0:T(8,128)} %fusion.105, f32[64,64,44,4,1]{1,2,4,3,0:T(8,128)} %fusion.108, bf16[64,14,4,64,1]{3,2,0,1,4:T(4,128)(2,1)} %bitcast.262, bf16[44,4,44,4]{2,0,1,3:T(8,128)(2,1)} %get-tuple-element.276), kind=kOutput, calls=%fused_computation.3.clone.1 | convolution fusion | flops 82903040 | bytes 15007744 | tf_op jit(solution)/shard_map/while/body/eval_jaxpr/niwpj,wpvq->nviqj/dot_general | solution.py:51
  432.0 6.3 %fusion.110 = bf16[44,64,4,64]{3,0,2,1:T(8,128)(2,1)S(1)} fusion(f32[64,64,44,4,1]{1,2,4,3,0:T(8,128)} %fusion.105, f32[64,64,44,4,1]{1,2,4,3,0:T(8,128)} %fusion.108, bf16[64,14,4,64,1]{3,2,0,1,4:T(4,128)(2,1)} %bitcast.262, bf16[44,4,44,4]{2,0,1,3:T(8,128)(2,1)} %get-tuple-element.276), kind=kOutput, calls=%fused_computation.3.clone.1 | convolution fusion | flops 82903040 | bytes 15007744 | tf_op jit(solution)/shard_map/while/body/eval_jaxpr/niwpj,wpvq->nviqj/dot_general | solution.py:51
  465.8 6.3 %fusion.110 = bf16[44,64,4,64]{3,0,2,1:T(8,128)(2,1)S(1)} fusion(f32[64,64,44,4,1]{1,2,4,3,0:T(8,128)} %fusion.105, f32[64,64,44,4,1]{1,2,4,3,0:T(8,128)} %fusion.108, bf16[64,14,4,64,1]{3,2,0,1,4:T(4,128)(2,1)} %bitcast.262, bf16[44,4,44,4]{2,0,1,3:T(8,128)(2,1)} %get-tuple-element.276), kind=kOutput, calls=%fused_computation.3.clone.1 | convolution fusion | flops 82903040 | bytes 15007744 | tf_op jit(solution)/shard_map/while/body/eval_jaxpr/niwpj,wpvq->nviqj/dot_general | solution.py:51
  499.6 6.3 %fusion.110 = bf16[44,64,4,64]{3,0,2,1:T(8,128)(2,1)S(1)} fusion(f32[64,64,44,4,1]{1,2,4,3,0:T(8,128)} %fusion.105, f32[64,64,44,4,1]{1,2,4,3,0:T(8,128)} %fusion.108, bf16[64,14,4,64,1]{3,2,0,1,4:T(4,128)(2,1)} %bitcast.262, bf16[44,4,44,4]{2,0,1,3:T(8,128)(2,1)} %get-tuple-element.276), kind=kOutput, calls=%fused_computation.3.clone.1 | convolution fusion | flops 82903040 | bytes 15007744 | tf_op jit(solution)/shard_map/while/body/eval_jaxpr/niwpj,wpvq->nviqj/dot_general | solution.py:51
  533.4 6.3 %fusion.110 = bf16[44,64,4,64]{3,0,2,1:T(8,128)(2,1)S(1)} fusion(f32[64,64,44,4,1]{1,2,4,3,0:T(8,128)} %fusion.105, f32[64,64,44,4,1]{1,2,4,3,0:T(8,128)} %fusion.108, bf16[64,14,4,64,1]{3,2,0,1,4:T(4,128)(2,1)} %bitcast.262, bf16[44,4,44,4]{2,0,1,3:T(8,128)(2,1)} %get-tuple-element.276), kind=kOutput, calls=%fused_computation.3.clone.1 | convolution fusion | flops 82903040 | bytes 15007744 | tf_op jit(solution)/shard_map/while/body/eval_jaxpr/niwpj,wpvq->nviqj/dot_general | solution.py:51
  567.2 6.3 %fusion.110 = bf16[44,64,4,64]{3,0,2,1:T(8,128)(2,1)S(1)} fusion(f32[64,64,44,4,1]{1,2,4,3,0:T(8,128)} %fusion.105, f32[64,64,44,4,1]{1,2,4,3,0:T(8,128)} %fusion.108, bf16[64,14,4,64,1]{3,2,0,1,4:T(4,128)(2,1)} %bitcast.262, bf16[44,4,44,4]{2,0,1,3:T(8,128)(2,1)} %get-tuple-element.276), kind=kOutput, calls=%fused_computation.3.clone.1 | convolution fusion | flops 82903040 | bytes 15007744 | tf_op jit(solution)/shard_map/while/body/eval_jaxpr/niwpj,wpvq->nviqj/dot_general | solution.py:51
  601.0 6.3 %fusion.110 = bf16[44,64,4,64]{3,0,2,1:T(8,128)(2,1)S(1)} fusion(f32[64,64,44,4,1]{1,2,4,3,0:T(8,128)} %fusion.105, f32[64,64,44,4,1]{1,2,4,3,0:T(8,128)} %fusion.108, bf16[64,14,4,64,1]{3,2,0,1,4:T(4,128)(2,1)} %bitcast.262, bf16[44,4,44,4]{2,0,1,3:T(8,128)(2,1)} %get-tuple-element.276), kind=kOutput, calls=%fused_computation.3.clone.1 | convolution fusion | flops 82903040 | bytes 15007744 | tf_op jit(solution)/shard_map/while/body/eval_jaxpr/niwpj,wpvq->nviqj/dot_general | solution.py:51
  (426 shorter events, 401.1 us)
Async XLA Ops:
  6.5 57.2 %copy-start.4 = (bf16[8,16,2816]{2,1,0:T(8,128)(2,1)S(1)}, bf16[8,16,2816]{2,1,0:T(8,128)(2,1)}, u32[]{:S(2)}) copy-start(bf16[8,16,2816]{2,1,0:T(8,128)(2,1)} %param.13) | copy-start | bytes 2162692
  6.5 339.1 %all-gather.2.cloned.1.call-start = ((), (), s32[]{:S(2)}) async-start(), calls=%async_computation | async-start | bytes 3604480 | tf_op jit(solution)/shard_map/all_gather | solution.py:78
  6.5 20.3 %collective-permute-start.2 = (bf16[8,16,2816]{2,1,0:T(8,128)(2,1)}, bf16[8,16,2816]{2,1,0:T(8,128)(2,1)S(1)}, u32[]{:S(2)}, u32[]{:S(2)}) collective-permute-start(bf16[8,16,2816]{2,1,0:T(8,128)(2,1)} %param.13), channel_id=1, source_target_pairs={{0,8},{8,16},{16,24},{24,0},{1,9},{9,17},{17,25},{25,1},{2,10},{10... | collective-permute-start | bytes 2162696 | tf_op jit(solution)/shard_map/ppermute | solution.py:12
  26.8 18.2 %collective-permute-start.3 = (bf16[8,16,2816]{2,1,0:T(8,128)(2,1)S(1)}, bf16[8,16,2816]{2,1,0:T(8,128)(2,1)S(1)}, u32[]{:S(2)}, u32[]{:S(2)}) collective-permute-start(bf16[8,16,2816]{2,1,0:T(8,128)(2,1)S(1)} %collective-permute-done.2), channel_id=1, source_target_pairs={{0,8},{8,16},{16,24},{24,0},{1,9},{9,17},{17,25},{25,1},{2,10},{10... | collective-permute-start | bytes 2162696 | tf_op jit(solution)/shard_map/ppermute | solution.py:12
  45.1 17.4 %collective-permute-start.4 = (bf16[8,16,2816]{2,1,0:T(8,128)(2,1)S(1)}, bf16[8,16,2816]{2,1,0:T(8,128)(2,1)}, u32[]{:S(2)}, u32[]{:S(2)}) collective-permute-start(bf16[8,16,2816]{2,1,0:T(8,128)(2,1)S(1)} %collective-permute-done.3), channel_id=1, source_target_pairs={{0,8},{8,16},{16,24},{24,0},{1,9},{9,17},{17,25},{25,1},{2,10},{10... | collective-permute-start | bytes 2162696 | tf_op jit(solution)/shard_map/ppermute | solution.py:12
  45.9 9.5 %collective-permute-start.1 = (bf16[2,1,64,256]{3,2,1,0:T(8,128)(2,1)S(1)}, bf16[2,1,64,256]{3,2,1,0:T(8,128)(2,1)S(1)}, u32[]{:S(2)}, u32[]{:S(2)}) collective-permute-start(bf16[2,1,64,256]{3,2,1,0:T(8,128)(2,1)S(1)} %get-tuple-element.146), channel_id=1, source_target_pairs={{1,0},{2,1},{3,2},{4,3},{5,4},{6,5},{7,6},{9,8},{10,9},{11,10},{12... | collective-permute-start | bytes 196616 | tf_op jit(solution)/shard_map/ppermute | solution.py:26
  47.2 8.2 %collective-permute-start = (bf16[2,1,64,256]{3,2,1,0:T(8,128)(2,1)S(1)}, bf16[2,1,64,256]{3,2,1,0:T(8,128)(2,1)S(1)}, u32[]{:S(2)}, u32[]{:S(2)}) collective-permute-start(bf16[2,1,64,256]{3,2,1,0:T(8,128)(2,1)S(1)} %get-tuple-element.145), channel_id=1, source_target_pairs={{0,1},{1,2},{2,3},{3,4},{4,5},{5,6},{6,7},{8,9},{9,10},{10,11},{11... | collective-permute-start | bytes 196616 | tf_op jit(solution)/shard_map/ppermute | solution.py:25
  102.5 5.6 copy-start
  137.2 5.6 copy-start
  172.0 5.6 copy-start
  206.7 5.6 copy-start
  241.5 5.6 copy-start
  276.2 5.6 copy-start
  310.9 5.6 copy-start
  346.5 270.3 %copy-start.5 = (pred[8,256]{1,0:T(8,128)(4,1)S(1)}, pred[8,256]{1,0:T(8,128)(4,1)}, u32[]{:S(2)}) copy-start(pred[8,256]{1,0:T(8,128)(4,1)} %broadcast_compare_fusion) | copy-start | bytes 6148
  346.5 270.3 %copy-start.6 = (pred[8,64]{1,0:T(8,128)(4,1)S(1)}, pred[8,64]{1,0:T(8,128)(4,1)}, u32[]{:S(2)}) copy-start(pred[8,64]{1,0:T(8,128)(4,1)} %iota_compare_fusion) | copy-start | bytes 1540
  346.5 5.7 copy-start.2
  380.2 5.8 copy-start.2
  414.0 5.8 copy-start.2
  447.8 5.8 copy-start.2
  481.6 5.8 copy-start.2
  515.4 5.8 copy-start.2
  549.3 5.8 copy-start.2
  583.1 5.8 copy-start.2
  (17 other events, 83.2 us)
Sparse Core Ops, SparseCore 0:
  50.4 43.3 all-gather.1
